TPU v7x, 32 devices: a whole 2x2x4 slice. The times are simulated.
32 devices in a mesh: blk: 8 (over z, x), head: 4 (over y, core).
Axes of the slice: x: 2, y: 2, z: 4, core: 2. Of those that a mesh axis runs over, the one named last changes fastest.
Arguments:
- queries: bfloat16 [4096, 1024], P(('blk', 'head')), may hold values from -6 to 6
- key_vectors: bfloat16 [4096, 1024], P(('blk', 'head')), may hold values from -6 to 6
- value_vectors: bfloat16 [4096, 1024], P(('blk', 'head')), may hold values from -6 to 6
- grad_output: bfloat16 [4096, 1024], P(('blk', 'head')), may hold values from -6 to 6
- lengths: int32 [4], replicated, may hold values from 1 to 2048, 4096 in all
Outputs:
- grad_queries: bfloat16 [4096, 1024], P(('blk', 'head'))
- grad_keys: bfloat16 [4096, 1024], P(('blk', 'head'))
- grad_values: bfloat16 [4096, 1024], P(('blk', 'head'))
Inputs may be any that keep to these rules, and one draw needn't show every extreme that they name: 4 positive lengths that sum to 4096; the longest is exactly 2048.
All inputs are finite; a program needn't handle non-finite values.
Results may differ from a plain program's by a relative error of at most 0.0086.
Values may be sent and summed in bfloat16 or wider, within the bound.
No kernel may reach another device: no remote copies, remote signals or barrier semaphores. Data moves between devices by JAX's collectives and lax.ppermute only.
A program may use at most 64 MiB of HBM per device.

v0:
```python
import jax
import jax.numpy as jnp
from jax import lax
from jax.sharding import PartitionSpec as P

DH = 64
WIN = 64


def with_halo(block, sides, width):
    for axis, dim in sides:
        count = lax.axis_size(axis)
        forward = [(i, i + 1) for i in range(count - 1)]
        backward = [(target, source) for source, target in forward]
        low = lax.ppermute(
            lax.slice_in_dim(block, block.shape[dim] - width, None, axis=dim), axis, forward
        )
        high = lax.ppermute(lax.slice_in_dim(block, 0, width, axis=dim), axis, backward)
        block = jnp.concatenate([low, block, high], axis=dim)
    return block


def shifted(block, axis, distance):
    devices = range(lax.axis_size(axis))
    route = [(i - distance, i) for i in devices if i - distance in devices]
    return lax.ppermute(block, axis, route)


def recording_of(positions, rec_ends):
    return jnp.sum((rec_ends[None, :] <= positions[:, None]).astype(jnp.int32), axis=1)


def band_grads(query_rows, grad_rows, key_value, query_first, key_first, rec_ends, frames):
    row_count = query_rows.shape[0]
    columns = query_rows.shape[1]
    head_count = columns // DH
    step_rows = min(512, 2 * WIN)
    key_span = step_rows + 2 * WIN
    score_scale = DH ** (-0.5)
    pair_grad = jnp.zeros((key_value.shape[0], 2 * columns), jnp.float32)
    query_parts = []
    for first_row in range(0, row_count, step_rows):
        query_block = query_rows[first_row : first_row + step_rows].reshape(
            step_rows, head_count, DH
        )
        grad_block = grad_rows[first_row : first_row + step_rows].reshape(step_rows, head_count, DH)
        pair_block = key_value[first_row : first_row + key_span]
        key_block = pair_block[:, :columns].reshape(key_span, head_count, DH)
        value_block = pair_block[:, columns:].reshape(key_span, head_count, DH)
        query_pos = query_first + first_row + jnp.arange(step_rows, dtype=jnp.int32)
        key_pos = key_first + first_row + jnp.arange(key_span, dtype=jnp.int32)
        inside = (key_pos >= 0) & (key_pos < frames)
        visible = jnp.abs(query_pos[:, None] - key_pos[None, :]) <= WIN
        visible = visible & (
            recording_of(query_pos, rec_ends)[:, None] == recording_of(key_pos, rec_ends)[None, :]
        )
        visible = visible & (inside[None, :] | (query_pos[:, None] == key_pos[None, :]))
        scores = (
            jnp.einsum("qhd,khd->hqk", query_block, key_block, preferred_element_type=jnp.float32)
            * score_scale
        )
        scores = jnp.where(visible[None], scores, -1e30)
        row_max = jnp.max(scores, axis=-1, keepdims=True)
        weights = jnp.where(visible[None], jnp.exp(scores - row_max), 0.0)
        probs = weights / jnp.sum(weights, axis=-1, keepdims=True)
        probs_low = probs.astype(jnp.bfloat16)
        value_part = jnp.einsum(
            "hqk,qhd->khd", probs_low, grad_block, preferred_element_type=jnp.float32
        )
        prob_grad = jnp.einsum(
            "qhd,khd->hqk", grad_block, value_block, preferred_element_type=jnp.float32
        )
        row_delta = jnp.sum(probs * prob_grad, axis=-1, keepdims=True)
        score_grad = (probs * (prob_grad - row_delta) * score_scale).astype(jnp.bfloat16)
        query_grad = jnp.einsum(
            "hqk,khd->qhd", score_grad, key_block, preferred_element_type=jnp.float32
        )
        key_part = jnp.einsum(
            "hqk,qhd->khd", score_grad, query_block, preferred_element_type=jnp.float32
        )
        both_parts = jnp.concatenate(
            [key_part.reshape(key_span, columns), value_part.reshape(key_span, columns)], axis=1
        )
        pair_grad = pair_grad.at[first_row : first_row + key_span].add(both_parts)
        query_parts.append(query_grad.reshape(step_rows, columns))
    return (jnp.concatenate(query_parts, axis=0), pair_grad)


def body(queries, key_vectors, value_vectors, grad_output, lengths):
    group_size = lax.axis_size("head")
    block_rows = queries.shape[0] * group_size
    columns = queries.shape[1] // group_size
    frames = block_rows * lax.axis_size("blk")
    head_queries, head_keys, head_values, head_grads = (
        lax.all_to_all(queries, "head", split_axis=1, concat_axis=0, tiled=True),
        lax.all_to_all(key_vectors, "head", split_axis=1, concat_axis=0, tiled=True),
        lax.all_to_all(value_vectors, "head", split_axis=1, concat_axis=0, tiled=True),
        lax.all_to_all(grad_output, "head", split_axis=1, concat_axis=0, tiled=True),
    )
    key_value = jnp.concatenate([head_keys, head_values], axis=1)
    rec_ends = jnp.cumsum(lengths)
    base_pos = lax.axis_index("blk") * block_rows
    extended = with_halo(key_value, (("blk", 0),), WIN)
    query_grad, pair_grad = band_grads(
        head_queries, head_grads, extended, base_pos, base_pos - WIN, rec_ends, frames
    )
    own_rows = pair_grad[WIN : WIN + block_rows]
    arrived = []
    for step_by, rim_rows in ((1, pair_grad[WIN + block_rows :]), (-1, pair_grad[:WIN])):
        arrived.append(shifted(rim_rows, "blk", step_by))
    own_rows = own_rows.at[:WIN].add(arrived[0]).at[block_rows - WIN :].add(arrived[1])
    outputs = (
        lax.all_to_all(
            query_grad.astype(jnp.bfloat16), "head", split_axis=0, concat_axis=1, tiled=True
        ),
        lax.all_to_all(
            own_rows[:, :columns].astype(jnp.bfloat16),
            "head",
            split_axis=0,
            concat_axis=1,
            tiled=True,
        ),
        lax.all_to_all(
            own_rows[:, columns:].astype(jnp.bfloat16),
            "head",
            split_axis=0,
            concat_axis=1,
            tiled=True,
        ),
    )
    return (outputs[0], outputs[1], outputs[2])


def solution(mesh):
    return jax.shard_map(
        body,
        mesh=mesh,
        in_specs=(
            P(("blk", "head"), None),
            P(("blk", "head"), None),
            P(("blk", "head"), None),
            P(("blk", "head"), None),
            P(),
        ),
        out_specs=(P(("blk", "head"), None), P(("blk", "head"), None), P(("blk", "head"), None)),
        check_vma=False,
    )
```

profile of v0, /device:TPU:26, one launch (start us, length us, event | category | flops | bytes accessed | tf_op | source)
XLA Modules:
  0.0 104.3 jit_solution(3987964290970095193)
XLA Ops:
  0.7 1.2 %copy.101 = bf16[128,1024]{0,1:T(8,128)(2,1)S(1)} copy(bf16[128,1024]{1,0:T(8,128)(2,1)} %param.18) | data formatting | bytes 524288 | tf_op args[1]
  1.8 0.9 copy.102
  2.7 3.4 %all-to-all-start = ((bf16[128,4,256]{2,0,1:T(8,128)(2,1)}), bf16[128,4,256]{2,0,1:T(8,128)(2,1)S(1)}, u32[]{:S(2)}, u32[]{:S(2)}) async-start(bf16[128,4,256]{2,0,1:T(8,128)(2,1)} %copy.102), calls=%async_computation | async-start | bytes 524288 | tf_op jit(solution)/shard_map/all_to_all | solution.py:96
  6.2 0.8 copy.156
  7.2 0.9 copy.104
  8.1 0.2 reduce-window.8
  8.4 0.2 fusion.87
  8.6 0.8 fusion.86
  9.4 2.7 %all-to-all-done = bf16[128,4,256]{2,0,1:T(8,128)(2,1)S(1)} async-done(((bf16[128,4,256]{2,0,1:T(8,128)(2,1)}), bf16[128,4,256]{2,0,1:T(8,128)(2,1)S(1)}, u32[]{:S(2)}, u32[]{:S(2)}) %all-to-all-start) | async-done | bytes 262176 | tf_op jit(solution)/shard_map/all_to_all | solution.py:96
  12.1 3.4 %all-to-all-start.1 = ((bf16[128,4,256]{2,0,1:T(8,128)(2,1)}), bf16[128,4,256]{2,0,1:T(8,128)(2,1)S(1)}, u32[]{:S(2)}, u32[]{:S(2)}) async-start(bf16[128,4,256]{2,0,1:T(8,128)(2,1)} %copy.104), calls=%async_computation.1 | async-start | bytes 524288 | tf_op jit(solution)/shard_map/all_to_all | solution.py:97
  15.5 0.8 fusion.85
  16.3 5.2 %all-to-all-done.1 = bf16[128,4,256]{2,0,1:T(8,128)(2,1)S(1)} async-done(((bf16[128,4,256]{2,0,1:T(8,128)(2,1)}), bf16[128,4,256]{2,0,1:T(8,128)(2,1)S(1)}, u32[]{:S(2)}, u32[]{:S(2)}) %all-to-all-start.1) | async-done | bytes 262176 | tf_op jit(solution)/shard_map/all_to_all | solution.py:97
  21.5 3.4 %all-to-all-start.2 = ((bf16[128,4,256]{0,2,1:T(8,128)(2,1)}), bf16[128,4,256]{0,2,1:T(8,128)(2,1)S(1)}, u32[]{:S(2)}, u32[]{:S(2)}) async-start(bf16[128,4,256]{0,2,1:T(8,128)(2,1)} %bitcast.9), calls=%async_computation.2 | async-start | bytes 524288 | tf_op jit(solution)/shard_map/all_to_all | solution.py:95
  24.9 0.2 fusion.84
  25.1 0.8 copy.157
  26.4 1.3 %collective-permute-start = (bf16[64,512]{0,1:T(8,128)(2,1)S(1)}, bf16[64,512]{0,1:T(8,128)(2,1)S(1)}, u32[]{:S(2)}, u32[]{:S(2)}) collective-permute-start(bf16[64,512]{0,1:T(8,128)(2,1)S(1)} %get-tuple-element.101), channel_id=1, source_target_pairs={{0,4},{4,8},{8,12},{12,16},{16,20},{20,24},{24,28},{1,5},{5,9},{9,... | collective-permute-start | bytes 196616 | tf_op jit(solution)/shard_map/ppermute | solution.py:15
  27.7 4.6 %collective-permute-start.1 = (bf16[64,512]{0,1:T(8,128)(2,1)S(1)}, bf16[64,512]{0,1:T(8,128)(2,1)S(1)}, u32[]{:S(2)}, u32[]{:S(2)}) collective-permute-start(bf16[64,512]{0,1:T(8,128)(2,1)S(1)} %get-tuple-element.102), channel_id=1, source_target_pairs={{4,0},{8,4},{12,8},{16,12},{20,16},{24,20},{28,24},{5,1},{9,5},{13... | collective-permute-start | bytes 196616 | tf_op jit(solution)/shard_map/ppermute | solution.py:18
  32.2 3.4 %all-to-all-start.3 = ((bf16[128,4,256]{0,2,1:T(8,128)(2,1)}), bf16[128,4,256]{0,2,1:T(8,128)(2,1)S(1)}, u32[]{:S(2)}, u32[]{:S(2)}) async-start(bf16[128,4,256]{0,2,1:T(8,128)(2,1)} %bitcast.14), calls=%async_computation.3 | async-start | bytes 524288 | tf_op jit(solution)/shard_map/all_to_all | solution.py:98
  35.7 6.0 %all-to-all-done.3 = bf16[128,4,256]{0,2,1:T(8,128)(2,1)S(1)} async-done(((bf16[128,4,256]{0,2,1:T(8,128)(2,1)}), bf16[128,4,256]{0,2,1:T(8,128)(2,1)S(1)}, u32[]{:S(2)}, u32[]{:S(2)}) %all-to-all-start.3) | async-done | bytes 262176 | tf_op jit(solution)/shard_map/all_to_all | solution.py:98
  41.7 0.5 pad_maximum_fusion.5
  42.3 0.3 convolution_bitcast_fusion.1
  42.5 0.4 fusion.123
  43.0 0.9 convolution_convert_fusion.3
  43.9 0.3 fusion.42
  44.2 0.6 fusion.70
  44.7 0.3 convolution_bitcast_fusion
  45.0 0.4 fusion.120
  45.4 0.9 convolution_convert_fusion.2
  46.4 1.0 fusion.45
  47.4 1.3 %fusion.64 = f32[4,256,64]{1,2,0:T(8,128)} fusion(bf16[128,4,64]{0,2,1:T(8,128)(2,1)S(1)} %bitcast.172, f32[4,128]{1,0:T(4,128)S(1)} %get-tuple-element.115, pred[128,256]{0,1:T(8,128)(4,1)S(1)} %fusion.84, bf16[256,4,64]{0,2,1:T(8,128)(2,1)S(1)} %bitcast.183, bf16[128,4,64]{0,2,1:T(8,128)(2,1)S(1)} %bitcast.197), kind=kOutput, calls=%fused_computation.78 | convolution fusion | flops 34341632 | bytes 559104 | tf_op jit(solution)/shard_map/hqk,qhd->khd/dot_general | solution.py:67
  48.7 0.3 fusion.125
  48.9 1.2 %fusion.121 = (f32[4,128]{1,0:T(4,128)S(1)}, f32[4,128,256]{1,2,0:T(8,128)}) fusion(bf16[128,4,64]{0,2,1:T(8,128)(2,1)S(1)} %bitcast.191, bf16[256,4,64]{0,2,1:T(8,128)(2,1)S(1)} %bitcast.178, pred[128,256]{0,1:T(8,128)(4,1)S(1)} %copy-done.16), kind=kOutput, calls=%fused_computation.172 | convolution fusion | flops 17432832 | bytes 755712 | tf_op jit(solution)/shard_map/sub | solution.py:64
  50.1 0.6 fusion.66
  50.7 0.3 fusion.124
  51.0 0.4 fusion.122
  51.4 1.3 %fusion.68 = f32[4,256,64]{1,2,0:T(8,128)} fusion(bf16[128,4,64]{0,2,1:T(8,128)(2,1)S(1)} %bitcast.168, f32[4,128]{1,0:T(4,128)S(1)} %get-tuple-element.119, pred[128,256]{0,1:T(8,128)(4,1)S(1)} %copy-done.15, bf16[128,4,64]{0,2,1:T(8,128)(2,1)S(1)} %bitcast.189, bf16[256,4,64]{0,2,1:T(8,128)(2,1)S(1)} %bitcast.176), kind=kOutput, calls=%fused_computation.82 | convolution fusion | flops 34341632 | bytes 559104 | tf_op jit(solution)/shard_map/hqk,qhd->khd/dot_general | solution.py:67
  52.7 1.5 %fusion.44 = f32[4,256,64]{1,2,0:T(8,128)S(1)} fusion(bf16[128,4,64]{0,2,1:T(8,128)(2,1)S(1)} %bitcast.193, f32[4,128,256]{1,2,0:T(8,128)S(1)} %fusion.125, f32[4,128,256]{1,2,0:T(8,128)} %get-tuple-element.118, f32[4,128]{1,0:T(4,128)S(1)} %get-tuple-element.117), kind=kOutput, calls=%fused_computation.56 | convolution fusion | flops 17695488 | bytes 1378304 | tf_op jit(solution)/shard_map/hqk,qhd->khd/dot_general | solution.py:78
  54.3 1.0 fusion.43
  55.4 0.9 copy-done.3
  56.5 0.7 copy-done.5
  57.3 0.2 constant_dynamic-update-slice_fusion
  57.6 1.3 %collective-permute-start.2 = (f32[64,512]{0,1:T(8,128)S(1)}, f32[64,512]{0,1:T(8,128)S(1)}, u32[]{:S(2)}, u32[]{:S(2)}) collective-permute-start(f32[64,512]{0,1:T(8,128)S(1)} %slice.255), channel_id=1, source_target_pairs={{0,4},{4,8},{8,12},{12,16},{16,20},{20,24},{24,28},{1,5},{5,9},{9,... | collective-permute-start | bytes 393224 | tf_op jit(solution)/shard_map/ppermute | solution.py:26
  59.0 1.5 %convolution_convert_fusion = bf16[4,128,64]{1,2,0:T(8,128)(2,1)S(1)} fusion(bf16[256,4,64]{0,2,1:T(8,128)(2,1)S(1)} %bitcast.180, f32[4,128,256]{1,2,0:T(8,128)S(1)} %fusion.125, f32[4,128,256]{1,2,0:T(8,128)} %get-tuple-element.118, f32[4,128]{1,0:T(4,128)S(1)} %get-tuple-element.117), kind=kOutput, calls=%fused_computation.50 | convolution fusion | flops 17728256 | bytes 1247232 | tf_op jit(solution)/shard_map/hqk,khd->qhd/dot_general | solution.py:75
  60.5 6.9 %collective-permute-done.2 = f32[64,512]{0,1:T(8,128)S(1)} collective-permute-done((f32[64,512]{0,1:T(8,128)S(1)}, f32[64,512]{0,1:T(8,128)S(1)}, u32[]{:S(2)}, u32[]{:S(2)}) %collective-permute-start.2) | collective-permute-done | bytes 131104 | tf_op jit(solution)/shard_map/ppermute | solution.py:26
  67.5 4.2 %collective-permute-start.3 = (f32[64,512]{0,1:T(8,128)S(1)}, f32[64,512]{0,1:T(8,128)S(1)}, u32[]{:S(2)}, u32[]{:S(2)}) collective-permute-start(f32[64,512]{0,1:T(8,128)S(1)} %get-tuple-element.91), channel_id=1, source_target_pairs={{4,0},{8,4},{12,8},{16,12},{20,16},{24,20},{28,24},{5,1},{9,5},{13... | collective-permute-start | bytes 393224 | tf_op jit(solution)/shard_map/ppermute | solution.py:26
  71.8 1.5 %convolution_convert_fusion.1 = bf16[4,128,64]{1,2,0:T(8,128)(2,1)S(1)} fusion(bf16[256,4,64]{0,2,1:T(8,128)(2,1)S(1)} %bitcast.177, f32[4,128,256]{1,2,0:T(8,128)S(1)} %fusion.124, f32[4,128,256]{1,2,0:T(8,128)} %copy-done.18, f32[4,128]{1,0:T(4,128)S(1)} %get-tuple-element.119), kind=kOutput, calls=%fused_computation.51 | convolution fusion | flops 17728256 | bytes 1247232 | tf_op jit(solution)/shard_map/hqk,khd->qhd/dot_general | solution.py:75
  73.3 0.3 slice.253
  73.6 0.5 copy-done.9
  74.2 0.8 copy.123
  75.0 3.4 %all-to-all-start.4 = ((bf16[4,128,256]{2,1,0:T(8,128)(2,1)}), bf16[4,128,256]{2,1,0:T(8,128)(2,1)S(1)}, u32[]{:S(2)}, u32[]{:S(2)}) async-start(bf16[4,128,256]{2,1,0:T(8,128)(2,1)} %bitcast.42), calls=%async_computation.4 | async-start | bytes 524288 | tf_op jit(solution)/shard_map/all_to_all | solution.py:113
  78.5 1.9 %scatter-add.26 = f32[512,512]{0,1:T(8,128)S(1)} dynamic-update-slice(f32[512,512]{0,1:T(8,128)S(1)} %slice.253, f32[64,512]{0,1:T(8,128)S(1)} %get-tuple-element.92, s32[]{:T(128)} %constant.187.clone.1, s32[]{:T(128)} %constant.187.clone.1) | dynamic-update-slice | bytes 262148 | tf_op jit(solution)/shard_map/scatter-add | solution.py:111
  80.5 1.5 %scatter-add.29 = f32[512,512]{0,1:T(8,128)S(1)} dynamic-update-slice(f32[512,512]{0,1:T(8,128)S(1)} %scatter-add.26, f32[64,512]{0,1:T(8,128)S(1)} %slice_add_fusion.3, s32[]{:T(128)} %constant.198.clone.1, s32[]{:T(128)} %constant.187.clone.1) | dynamic-update-slice | bytes 262148 | tf_op jit(solution)/shard_map/scatter-add | solution.py:111
  82.1 0.8 copy.135
  83.0 1.5 %all-to-all-done.4 = bf16[4,128,256]{2,1,0:T(8,128)(2,1)S(1)} async-done(((bf16[4,128,256]{2,1,0:T(8,128)(2,1)}), bf16[4,128,256]{2,1,0:T(8,128)(2,1)S(1)}, u32[]{:S(2)}, u32[]{:S(2)}) %all-to-all-start.4) | async-done | bytes 262176 | tf_op jit(solution)/shard_map/all_to_all | solution.py:113
  84.5 3.4 %all-to-all-start.6 = ((bf16[4,128,256]{2,1,0:T(8,128)(2,1)}), bf16[4,128,256]{2,1,0:T(8,128)(2,1)S(1)}, u32[]{:S(2)}, u32[]{:S(2)}) async-start(bf16[4,128,256]{2,1,0:T(8,128)(2,1)} %bitcast.64), calls=%async_computation.6 | async-start | bytes 524288 | tf_op jit(solution)/shard_map/all_to_all | solution.py:123
  87.9 0.8 copy.133
  88.7 5.2 %all-to-all-done.6 = bf16[4,128,256]{2,1,0:T(8,128)(2,1)S(1)} async-done(((bf16[4,128,256]{2,1,0:T(8,128)(2,1)}), bf16[4,128,256]{2,1,0:T(8,128)(2,1)S(1)}, u32[]{:S(2)}, u32[]{:S(2)}) %all-to-all-start.6) | async-done | bytes 262176 | tf_op jit(solution)/shard_map/all_to_all | solution.py:123
  93.9 3.4 %all-to-all-start.5 = ((bf16[4,128,256]{2,1,0:T(8,128)(2,1)}), bf16[4,128,256]{2,1,0:T(8,128)(2,1)S(1)}, u32[]{:S(2)}, u32[]{:S(2)}) async-start(bf16[4,128,256]{2,1,0:T(8,128)(2,1)} %bitcast.61), calls=%async_computation.5 | async-start | bytes 524288 | tf_op jit(solution)/shard_map/all_to_all | solution.py:116
  97.3 0.2 copy.124
  97.5 0.9 copy.137
  98.5 0.9 copy.139
  99.4 3.9 %all-to-all-done.5 = bf16[4,128,256]{2,1,0:T(8,128)(2,1)S(1)} async-done(((bf16[4,128,256]{2,1,0:T(8,128)(2,1)}), bf16[4,128,256]{2,1,0:T(8,128)(2,1)S(1)}, u32[]{:S(2)}, u32[]{:S(2)}) %all-to-all-start.5) | async-done | bytes 262176 | tf_op jit(solution)/shard_map/all_to_all | solution.py:116
  103.3 0.2 copy.134
  103.5 0.9 copy.138
  (63 shorter events, 2.1 us)
Async XLA Ops:
  0.6 5.6 %copy-start = (bf16[128,1024]{1,0:T(8,128)(2,1)S(1)}, bf16[128,1024]{1,0:T(8,128)(2,1)}, u32[]{:S(2)}) copy-start(bf16[128,1024]{1,0:T(8,128)(2,1)} %param.17) | copy-start | bytes 786436
  0.6 6.4 %copy-start.1 = (bf16[128,1024]{1,0:T(8,128)(2,1)S(1)}, bf16[128,1024]{1,0:T(8,128)(2,1)}, u32[]{:S(2)}) copy-start(bf16[128,1024]{1,0:T(8,128)(2,1)} %param.19) | copy-start | bytes 786436
  1.8 6.3 %copy-start.17 = (s32[4]{0:T(128)S(1)}, s32[4]{0:T(128)}, u32[]{:S(2)}) copy-start(s32[4]{0:T(128)} %param.21) | copy-start | bytes 52
  2.7 9.4 %all-to-all-start = ((bf16[128,4,256]{2,0,1:T(8,128)(2,1)}), bf16[128,4,256]{2,0,1:T(8,128)(2,1)S(1)}, u32[]{:S(2)}, u32[]{:S(2)}) async-start(bf16[128,4,256]{2,0,1:T(8,128)(2,1)} %copy.102), calls=%async_computation | async-start | bytes 524288 | tf_op jit(solution)/shard_map/all_to_all | solution.py:96
  6.2 18.9 %copy-start.2 = (bf16[128,1024]{1,0:T(8,128)(2,1)S(1)}, bf16[128,1024]{1,0:T(8,128)(2,1)}, u32[]{:S(2)}) copy-start(bf16[128,1024]{1,0:T(8,128)(2,1)} %param.20) | copy-start | bytes 786436
  12.1 9.4 %all-to-all-start.1 = ((bf16[128,4,256]{2,0,1:T(8,128)(2,1)}), bf16[128,4,256]{2,0,1:T(8,128)(2,1)S(1)}, u32[]{:S(2)}, u32[]{:S(2)}) async-start(bf16[128,4,256]{2,0,1:T(8,128)(2,1)} %copy.104), calls=%async_computation.1 | async-start | bytes 524288 | tf_op jit(solution)/shard_map/all_to_all | solution.py:97
  21.5 10.7 %all-to-all-start.2 = ((bf16[128,4,256]{0,2,1:T(8,128)(2,1)}), bf16[128,4,256]{0,2,1:T(8,128)(2,1)S(1)}, u32[]{:S(2)}, u32[]{:S(2)}) async-start(bf16[128,4,256]{0,2,1:T(8,128)(2,1)} %bitcast.9), calls=%async_computation.2 | async-start | bytes 524288 | tf_op jit(solution)/shard_map/all_to_all | solution.py:95
  26.4 15.3 %collective-permute-start = (bf16[64,512]{0,1:T(8,128)(2,1)S(1)}, bf16[64,512]{0,1:T(8,128)(2,1)S(1)}, u32[]{:S(2)}, u32[]{:S(2)}) collective-permute-start(bf16[64,512]{0,1:T(8,128)(2,1)S(1)} %get-tuple-element.101), channel_id=1, source_target_pairs={{0,4},{4,8},{8,12},{12,16},{16,20},{20,24},{24,28},{1,5},{5,9},{9,... | collective-permute-start | bytes 196616 | tf_op jit(solution)/shard_map/ppermute | solution.py:15
  27.7 14.0 %collective-permute-start.1 = (bf16[64,512]{0,1:T(8,128)(2,1)S(1)}, bf16[64,512]{0,1:T(8,128)(2,1)S(1)}, u32[]{:S(2)}, u32[]{:S(2)}) collective-permute-start(bf16[64,512]{0,1:T(8,128)(2,1)S(1)} %get-tuple-element.102), channel_id=1, source_target_pairs={{4,0},{8,4},{12,8},{16,12},{20,16},{24,20},{28,24},{5,1},{9,5},{13... | collective-permute-start | bytes 196616 | tf_op jit(solution)/shard_map/ppermute | solution.py:18
  32.2 9.4 %all-to-all-start.3 = ((bf16[128,4,256]{0,2,1:T(8,128)(2,1)}), bf16[128,4,256]{0,2,1:T(8,128)(2,1)S(1)}, u32[]{:S(2)}, u32[]{:S(2)}) async-start(bf16[128,4,256]{0,2,1:T(8,128)(2,1)} %bitcast.14), calls=%async_computation.3 | async-start | bytes 524288 | tf_op jit(solution)/shard_map/all_to_all | solution.py:98
  35.7 14.4 %copy-start.12 = (bf16[1,128,256]{1,2,0:T(8,128)(2,1)}, bf16[1,128,256]{1,2,0:T(8,128)(2,1)S(1)}, u32[]{:S(2)}) copy-start(bf16[1,128,256]{1,2,0:T(8,128)(2,1)S(1)} %get-tuple-element.105) | copy-start | bytes 196612
  35.7 15.7 %copy-start.10 = (bf16[1,128,256]{1,2,0:T(8,128)(2,1)}, bf16[1,128,256]{1,2,0:T(8,128)(2,1)S(1)}, u32[]{:S(2)}) copy-start(bf16[1,128,256]{1,2,0:T(8,128)(2,1)S(1)} %get-tuple-element.106) | copy-start | bytes 196612
  42.3 7.9 %copy-start.7 = (bf16[256,256]{0,1:T(8,128)(2,1)}, bf16[256,256]{0,1:T(8,128)(2,1)S(1)}, u32[]{:S(2)}) copy-start(bf16[256,256]{0,1:T(8,128)(2,1)S(1)} %get-tuple-element.111) | copy-start | bytes 393220
  47.4 1.6 %copy-start.16 = (pred[128,256]{0,1:T(8,128)(4,1)S(1)}, pred[128,256]{0,1:T(8,128)(4,1)}, u32[]{:S(2)}) copy-start(pred[128,256]{0,1:T(8,128)(4,1)} %fusion.85) | copy-start | bytes 98308
  50.1 0.9 copy-start.15
  51.4 2.8 %copy-start.18 = (f32[4,128,256]{1,2,0:T(8,128)}, f32[4,128,256]{1,2,0:T(8,128)S(1)}, u32[]{:S(2)}) copy-start(f32[4,128,256]{1,2,0:T(8,128)S(1)} %get-tuple-element.120) | copy-start | bytes 1572868
  51.4 1.3 %copy-start.13 = (bf16[1,128,256]{1,2,0:T(8,128)(2,1)S(1)}, bf16[1,128,256]{1,2,0:T(8,128)(2,1)}, u32[]{:S(2)}) copy-start(bf16[1,128,256]{1,2,0:T(8,128)(2,1)} %copy-done.12) | copy-start | bytes 196612
  52.7 1.6 %copy-start.11 = (bf16[1,128,256]{1,2,0:T(8,128)(2,1)S(1)}, bf16[1,128,256]{1,2,0:T(8,128)(2,1)}, u32[]{:S(2)}) copy-start(bf16[1,128,256]{1,2,0:T(8,128)(2,1)} %copy-done.10) | copy-start | bytes 196612
  55.3 0.9 copy-start.3
  55.3 1.0 copy-start.4
  56.3 0.9 copy-start.5
  56.3 1.0 copy-start.6
  57.3 1.6 %copy-start.8 = (bf16[256,256]{0,1:T(8,128)(2,1)S(1)}, bf16[256,256]{0,1:T(8,128)(2,1)}, u32[]{:S(2)}) copy-start(bf16[256,256]{0,1:T(8,128)(2,1)} %copy-done.7) | copy-start | bytes 393220
  57.6 9.7 %collective-permute-start.2 = (f32[64,512]{0,1:T(8,128)S(1)}, f32[64,512]{0,1:T(8,128)S(1)}, u32[]{:S(2)}, u32[]{:S(2)}) collective-permute-start(f32[64,512]{0,1:T(8,128)S(1)} %slice.255), channel_id=1, source_target_pairs={{0,4},{4,8},{8,12},{12,16},{16,20},{20,24},{24,28},{1,5},{5,9},{9,... | collective-permute-start | bytes 393224 | tf_op jit(solution)/shard_map/ppermute | solution.py:26
  67.5 12.9 %collective-permute-start.3 = (f32[64,512]{0,1:T(8,128)S(1)}, f32[64,512]{0,1:T(8,128)S(1)}, u32[]{:S(2)}, u32[]{:S(2)}) collective-permute-start(f32[64,512]{0,1:T(8,128)S(1)} %get-tuple-element.91), channel_id=1, source_target_pairs={{4,0},{8,4},{12,8},{16,12},{20,16},{24,20},{28,24},{5,1},{9,5},{13... | collective-permute-start | bytes 393224 | tf_op jit(solution)/shard_map/ppermute | solution.py:26
  73.3 0.8 copy-start.9
  73.3 0.9 copy-start.14
  75.0 9.4 %all-to-all-start.4 = ((bf16[4,128,256]{2,1,0:T(8,128)(2,1)}), bf16[4,128,256]{2,1,0:T(8,128)(2,1)S(1)}, u32[]{:S(2)}, u32[]{:S(2)}) async-start(bf16[4,128,256]{2,1,0:T(8,128)(2,1)} %bitcast.42), calls=%async_computation.4 | async-start | bytes 524288 | tf_op jit(solution)/shard_map/all_to_all | solution.py:113
  84.5 9.4 %all-to-all-start.6 = ((bf16[4,128,256]{2,1,0:T(8,128)(2,1)}), bf16[4,128,256]{2,1,0:T(8,128)(2,1)S(1)}, u32[]{:S(2)}, u32[]{:S(2)}) async-start(bf16[4,128,256]{2,1,0:T(8,128)(2,1)} %bitcast.64), calls=%async_computation.6 | async-start | bytes 524288 | tf_op jit(solution)/shard_map/all_to_all | solution.py:123
  93.9 9.4 %all-to-all-start.5 = ((bf16[4,128,256]{2,1,0:T(8,128)(2,1)}), bf16[4,128,256]{2,1,0:T(8,128)(2,1)S(1)}, u32[]{:S(2)}, u32[]{:S(2)}) async-start(bf16[4,128,256]{2,1,0:T(8,128)(2,1)} %bitcast.61), calls=%async_computation.5 | async-start | bytes 524288 | tf_op jit(solution)/shard_map/all_to_all | solution.py:116
where the time goes:
time: 105 us; the launch traced here: 104 us
  starting transfers between devices  35.2 us (34%)
  waiting for transfers between devices  31.4 us (30%)
  local copies, waits for them, and re-layouts  16.8 us (16%)
  matrix products  15.9 us (15%)
  other arithmetic  3.8 us (4%)
  between operations  1.16 us (1%)
    ppermute x2, waiting for transfers between devices, shifted(): return lax.ppermute(block, axis, route)  6.94 us
    unnamed x43, local copies, waits for them, and re-layouts  6.22 us
    all_to_all x1, waiting for transfers between devices, body(): lax.all_to_all(grad_output, 'head', split_axis=1, concat_axis=0, tiled=True)  5.95 us
    ppermute x2, starting transfers between devices, shifted(): return lax.ppermute(block, axis, route)  5.54 us
    all_to_all x1, waiting for transfers between devices, body(): lax.all_to_all(value_vectors, 'head', split_axis=1, concat_axis=0, tiled=...  5.22 us
    all_to_all x1, waiting for transfers between devices, body(): lax.all_to_all(own_rows[:, columns:].astype(jnp.bfloat16), 'head', split_...  5.16 us
    dot_general x4, matrix products, band_grads(): jnp.einsum('hqk,khd->qhd', score_grad, key_block, preferred_element_type=...  4.84 us
    ppermute x1, starting transfers between devices, with_halo(): lax.ppermute(lax.slice_in_dim(block, 0, width, axis=dim), axis, backward)  4.55 us
  transfers between devices with their start and end apart: 11, of which 7 were waited for; matrix products, arithmetic and copies ran while one was open for 16% of the time, Pallas kernels for 0%

commit v1 on v0

--- a/solution.py
+++ b/solution.py
@@ -5,6 +5,22 @@
 
 DH = 64
 WIN = 64
+
+
+def pairwise_exchange(x, axis, split, join):
+    ways, here = (lax.axis_size(axis), lax.axis_index(axis))
+    width = x.shape[split] // ways
+    dims = list(x.shape)
+    dims[split] = width
+    height = dims[join]
+    dims[join] = height * ways
+    full = jnp.zeros(dims, x.dtype)
+    for mask in range(ways):
+        part = lax.dynamic_slice_in_dim(x, (here ^ mask) * width, width, axis=split)
+        if mask:
+            part = lax.ppermute(part, axis, [(d, d ^ mask) for d in range(ways)])
+        full = lax.dynamic_update_slice_in_dim(full, part, (here ^ mask) * height, axis=join)
+    return full
 
 
 def with_halo(block, sides, width):
@@ -120,13 +136,7 @@
             concat_axis=1,
             tiled=True,
         ),
-        lax.all_to_all(
-            own_rows[:, columns:].astype(jnp.bfloat16),
-            "head",
-            split_axis=0,
-            concat_axis=1,
-            tiled=True,
-        ),
+        pairwise_exchange(own_rows[:, columns:].astype(jnp.bfloat16), "head", 0, 1),
     )
     return (outputs[0], outputs[1], outputs[2])
 

time: 105 us -> 93.8 us (0.89)
  local copies, waits for them, and re-layouts: 16.8 us -> 10.6 us
  waiting for transfers between devices: 31.4 us -> 28.2 us
  matrix products: 15.9 us -> 13.8 us
    ppermute x0 -> x3, waiting for transfers between devices: none -> 6.68 us  [pairwise_exchange(): part = lax.ppermute(part, axis, [(d, d ^ mask) for d in range(ways)])]
    all_to_all x1 -> x0, waiting for transfers between devices: 5.16 us -> none  [body(): lax.all_to_all(own_rows[:, columns:].astype(jnp.bfloat16), 'head', split_...]
    all_to_all x1, waiting for transfers between devices: 3.94 us -> 0.01 us  [body(): lax.all_to_all(own_rows[:, :columns].astype(jnp.bfloat16), 'head', split_...]
    unnamed x43 -> x35, local copies, waits for them, and re-layouts: 6.22 us -> 2.51 us
    all_to_all x1 -> x0, starting transfers between devices: 3.41 us -> none  [body(): lax.all_to_all(own_rows[:, columns:].astype(jnp.bfloat16), 'head', split_...]
    scatter-add x2 -> x0, local copies, waits for them, and re-layouts: 3.37 us -> none  [body(): own_rows.at[:WIN].add(arrived[0]).at[block_rows - WIN:].add(arrived[1])]
    ppermute x2, waiting for transfers between devices: 6.94 us -> 3.71 us  [shifted(): return lax.ppermute(block, axis, route)]
    all_to_all x1, waiting for transfers between devices: 1.49 us -> 4.55 us  [body(): lax.all_to_all(query_grad.astype(jnp.bfloat16), 'head', split_axis=0, con...]
  transfers between devices with their start and end apart: 11 -> 13, of which waited for: 7 -> 6; matrix products, arithmetic and copies ran while one was open for 16% -> 14% of each run, Pallas kernels for 0% -> 0%
where the time goes in v1:
time: 93.8 us; the launch traced here: 92.9 us
  starting transfers between devices  34.7 us (37%)
  waiting for transfers between devices  28.2 us (30%)
  matrix products  13.8 us (15%)
  local copies, waits for them, and re-layouts  10.6 us (11%)
  other arithmetic  4.36 us (5%)
  between operations  1.27 us (1%)
    ppermute x3, waiting for transfers between devices, pairwise_exchange(): part = lax.ppermute(part, axis, [(d, d ^ mask) for d in range(ways)])  6.68 us
    ppermute x2, starting transfers between devices, shifted(): return lax.ppermute(block, axis, route)  5.8 us
    dot_general x4, matrix products, band_grads(): jnp.einsum('hqk,khd->qhd', score_grad, key_block, preferred_element_type=...  5.55 us
    all_to_all x1, waiting for transfers between devices, body(): lax.all_to_all(grad_output, 'head', split_axis=1, concat_axis=0, tiled=True)  5.33 us
    all_to_all x1, waiting for transfers between devices, body(): lax.all_to_all(value_vectors, 'head', split_axis=1, concat_axis=0, tiled=...  5.23 us
    ppermute x1, starting transfers between devices, with_halo(): lax.ppermute(lax.slice_in_dim(block, 0, width, axis=dim), axis, backward)  4.55 us
    all_to_all x1, waiting for transfers between devices, body(): lax.all_to_all(query_grad.astype(jnp.bfloat16), 'head', split_axis=0, con...  4.55 us
    ppermute x2, waiting for transfers between devices, shifted(): return lax.ppermute(block, axis, route)  3.71 us
  transfers between devices with their start and end apart: 13, of which 6 were waited for; matrix products, arithmetic and copies ran while one was open for 14% of the time, Pallas kernels for 0%

profile of v1, /device:TPU:26, one launch (start us, length us, event | category | flops | bytes accessed | tf_op | source)
XLA Modules:
  0.0 92.9 jit_solution(5158475037763423554)
XLA Ops:
  0.7 1.2 %copy.118 = bf16[128,1024]{0,1:T(8,128)(2,1)S(1)} copy(bf16[128,1024]{1,0:T(8,128)(2,1)} %param.18) | data formatting | bytes 524288 | tf_op args[1]
  1.8 0.9 copy.119
  2.7 3.4 %all-to-all-start = ((bf16[128,4,256]{2,0,1:T(8,128)(2,1)}), bf16[128,4,256]{2,0,1:T(8,128)(2,1)S(1)}, u32[]{:S(2)}, u32[]{:S(2)}) async-start(bf16[128,4,256]{2,0,1:T(8,128)(2,1)} %copy.119), calls=%async_computation | async-start | bytes 524288 | tf_op jit(solution)/shard_map/all_to_all | solution.py:112
  6.2 0.8 copy.176
  7.1 0.2 copy.120
  7.2 0.9 copy.121
  8.1 0.2 reduce-window.8
  8.5 0.2 fusion.89
  8.6 0.8 fusion.88
  9.4 2.7 %all-to-all-done = bf16[128,4,256]{2,0,1:T(8,128)(2,1)S(1)} async-done(((bf16[128,4,256]{2,0,1:T(8,128)(2,1)}), bf16[128,4,256]{2,0,1:T(8,128)(2,1)S(1)}, u32[]{:S(2)}, u32[]{:S(2)}) %all-to-all-start) | async-done | bytes 262176 | tf_op jit(solution)/shard_map/all_to_all | solution.py:112
  12.1 3.4 %all-to-all-start.1 = ((bf16[128,4,256]{2,0,1:T(8,128)(2,1)}), bf16[128,4,256]{2,0,1:T(8,128)(2,1)S(1)}, u32[]{:S(2)}, u32[]{:S(2)}) async-start(bf16[128,4,256]{2,0,1:T(8,128)(2,1)} %copy.121), calls=%async_computation.1 | async-start | bytes 524288 | tf_op jit(solution)/shard_map/all_to_all | solution.py:113
  15.5 0.8 fusion.87
  16.3 5.2 %all-to-all-done.1 = bf16[128,4,256]{2,0,1:T(8,128)(2,1)S(1)} async-done(((bf16[128,4,256]{2,0,1:T(8,128)(2,1)}), bf16[128,4,256]{2,0,1:T(8,128)(2,1)S(1)}, u32[]{:S(2)}, u32[]{:S(2)}) %all-to-all-start.1) | async-done | bytes 262176 | tf_op jit(solution)/shard_map/all_to_all | solution.py:113
  21.5 3.4 %all-to-all-start.2 = ((bf16[128,4,256]{0,2,1:T(8,128)(2,1)}), bf16[128,4,256]{0,2,1:T(8,128)(2,1)S(1)}, u32[]{:S(2)}, u32[]{:S(2)}) async-start(bf16[128,4,256]{0,2,1:T(8,128)(2,1)} %bitcast.9), calls=%async_computation.2 | async-start | bytes 524288 | tf_op jit(solution)/shard_map/all_to_all | solution.py:111
  24.9 0.2 fusion.86
  25.1 0.8 copy.177
  26.0 0.1 copy.122
  26.1 0.1 copy.123
  26.4 1.3 %collective-permute-start = (bf16[64,512]{0,1:T(8,128)(2,1)S(1)}, bf16[64,512]{0,1:T(8,128)(2,1)S(1)}, u32[]{:S(2)}, u32[]{:S(2)}) collective-permute-start(bf16[64,512]{0,1:T(8,128)(2,1)S(1)} %get-tuple-element.101), channel_id=1, source_target_pairs={{0,4},{4,8},{8,12},{12,16},{16,20},{20,24},{24,28},{1,5},{5,9},{9,... | collective-permute-start | bytes 196616 | tf_op jit(solution)/shard_map/ppermute | solution.py:31
  27.7 4.6 %collective-permute-start.1 = (bf16[64,512]{0,1:T(8,128)(2,1)S(1)}, bf16[64,512]{0,1:T(8,128)(2,1)S(1)}, u32[]{:S(2)}, u32[]{:S(2)}) collective-permute-start(bf16[64,512]{0,1:T(8,128)(2,1)S(1)} %get-tuple-element.102), channel_id=1, source_target_pairs={{4,0},{8,4},{12,8},{16,12},{20,16},{24,20},{28,24},{5,1},{9,5},{13... | collective-permute-start | bytes 196616 | tf_op jit(solution)/shard_map/ppermute | solution.py:34
  32.3 3.4 %all-to-all-start.3 = ((bf16[128,4,256]{0,2,1:T(8,128)(2,1)}), bf16[128,4,256]{0,2,1:T(8,128)(2,1)S(1)}, u32[]{:S(2)}, u32[]{:S(2)}) async-start(bf16[128,4,256]{0,2,1:T(8,128)(2,1)} %bitcast.14), calls=%async_computation.3 | async-start | bytes 524288 | tf_op jit(solution)/shard_map/all_to_all | solution.py:114
  35.7 0.7 fusion.120
  36.4 5.3 %all-to-all-done.3 = bf16[128,4,256]{0,2,1:T(8,128)(2,1)S(1)} async-done(((bf16[128,4,256]{0,2,1:T(8,128)(2,1)}), bf16[128,4,256]{0,2,1:T(8,128)(2,1)S(1)}, u32[]{:S(2)}, u32[]{:S(2)}) %all-to-all-start.3) | async-done | bytes 262176 | tf_op jit(solution)/shard_map/all_to_all | solution.py:114
  41.7 1.2 %pad_maximum_fusion.5 = (bf16[256,256]{0,1:T(8,128)(2,1)S(1)}, bf16[256,256]{0,1:T(8,128)(2,1)S(1)}, bf16[256,256]{0,1:T(8,128)(2,1)S(1)}, bf16[256,256]{0,1:T(8...) fusion(bf16[64,512]{0,1:T(8,128)(2,1)S(1)} %collective-permute-, ...), kind=kLoop, calls=%fused_computation.104 | loop fusion | flops 1572864 | bytes 2359296 | tf_op jit(solution)/shard_map/concatenate | solution.py:35
  42.9 0.3 convolution_bitcast_fusion.1
  43.2 0.4 fusion.125
  43.6 0.9 convolution_convert_fusion.3
  44.5 0.3 fusion.42
  44.8 0.6 fusion.70
  45.4 0.3 convolution_bitcast_fusion
  45.7 0.4 fusion.122
  46.1 0.9 convolution_convert_fusion.2
  47.0 0.3 fusion.45
  47.3 0.6 fusion.64
  48.4 0.3 fusion.127
  48.8 0.4 fusion.123
  49.2 0.6 fusion.66
  50.0 0.3 fusion.44
  50.4 0.3 fusion.126
  50.9 1.2 %fusion.124 = (f32[4,128]{1,0:T(4,128)S(1)}, f32[4,128,256]{1,2,0:T(8,128)}) fusion(bf16[128,4,64]{0,2,1:T(8,128)(2,1)S(1)} %bitcast.184, bf16[256,4,64]{0,2,1:T(8,128)(2,1)S(1)} %bitcast.171, pred[128,256]{0,1:T(8,128)(4,1)S(1)} %copy-done.12), kind=kOutput, calls=%fused_computation.182 | convolution fusion | flops 17432832 | bytes 755712 | tf_op jit(solution)/shard_map/sub | solution.py:80
  52.0 0.6 fusion.68
  52.6 0.1 copy.149
  52.8 1.5 %fusion.43 = f32[4,256,64]{1,2,0:T(8,128)S(1)} fusion(bf16[128,4,64]{0,2,1:T(8,128)(2,1)S(1)} %bitcast.186, f32[4,128,256]{1,2,0:T(8,128)S(1)} %fusion.126, f32[4,128,256]{1,2,0:T(8,128)} %get-tuple-element.124, f32[4,128]{1,0:T(4,128)S(1)} %get-tuple-element.123), kind=kOutput, calls=%fused_computation.55 | convolution fusion | flops 17695488 | bytes 1378304 | tf_op jit(solution)/shard_map/hqk,qhd->khd/dot_general | solution.py:94
  54.5 0.2 select_maximum_fusion
  54.6 0.1 fusion.63
  54.8 0.1 fusion.62
  54.9 0.2 constant_dynamic-update-slice_fusion.3
  55.1 1.4 %collective-permute-start.2 = (f32[64,512]{1,0:T(8,128)S(1)}, f32[64,512]{1,0:T(8,128)S(1)}, u32[]{:S(2)}, u32[]{:S(2)}) collective-permute-start(f32[64,512]{1,0:T(8,128)S(1)} %slice.255), channel_id=1, source_target_pairs={{0,4},{4,8},{8,12},{12,16},{16,20},{20,24},{24,28},{1,5},{5,9},{9,... | collective-permute-start | bytes 393224 | tf_op jit(solution)/shard_map/ppermute | solution.py:42
  56.7 1.8 %convolution_convert_fusion = bf16[4,128,64]{1,2,0:T(8,128)(2,1)S(1)} fusion(bf16[256,4,64]{0,2,1:T(8,128)(2,1)S(1)} %bitcast.176, f32[4,128,256]{1,2,0:T(8,128)} %copy-done.1, f32[4,128,256]{1,2,0:T(8,128)} %copy-done.15, f32[4,128]{1,0:T(4,128)S(1)} %get-tuple-element.121), kind=kOutput, calls=%fused_computation.50 | convolution fusion | flops 17728256 | bytes 1247232 | tf_op jit(solution)/shard_map/hqk,khd->qhd/dot_general | solution.py:91
  58.5 3.7 %collective-permute-done.2 = f32[64,512]{1,0:T(8,128)S(1)} collective-permute-done((f32[64,512]{1,0:T(8,128)S(1)}, f32[64,512]{1,0:T(8,128)S(1)}, u32[]{:S(2)}, u32[]{:S(2)}) %collective-permute-start.2) | collective-permute-done | bytes 131104 | tf_op jit(solution)/shard_map/ppermute | solution.py:42
  62.2 4.4 %collective-permute-start.3 = (f32[64,512]{1,0:T(8,128)S(1)}, f32[64,512]{1,0:T(8,128)S(1)}, u32[]{:S(2)}, u32[]{:S(2)}) collective-permute-start(f32[64,512]{1,0:T(8,128)S(1)} %get-tuple-element.91), channel_id=1, source_target_pairs={{4,0},{8,4},{12,8},{16,12},{20,16},{24,20},{28,24},{5,1},{9,5},{13... | collective-permute-start | bytes 393224 | tf_op jit(solution)/shard_map/ppermute | solution.py:42
  66.6 1.9 %convolution_convert_fusion.1 = bf16[4,128,64]{1,2,0:T(8,128)(2,1)S(1)} fusion(bf16[256,4,64]{0,2,1:T(8,128)(2,1)S(1)} %bitcast.173, f32[4,128,256]{1,2,0:T(8,128)} %copy-done, f32[4,128,256]{1,2,0:T(8,128)} %get-tuple-element.124, f32[4,128]{1,0:T(4,128)S(1)} %get-tuple-element.123), kind=kOutput, calls=%fused_computation.51 | convolution fusion | flops 17728256 | bytes 1247232 | tf_op jit(solution)/shard_map/hqk,khd->qhd/dot_general | solution.py:91
  68.6 0.8 copy.140
  69.4 3.4 %all-to-all-start.4 = ((bf16[4,128,256]{2,1,0:T(8,128)(2,1)}), bf16[4,128,256]{2,1,0:T(8,128)(2,1)S(1)}, u32[]{:S(2)}, u32[]{:S(2)}) async-start(bf16[4,128,256]{2,1,0:T(8,128)(2,1)} %bitcast.42), calls=%async_computation.4 | async-start | bytes 524288 | tf_op jit(solution)/shard_map/all_to_all | solution.py:129
  73.0 0.7 fusion.119
  73.8 0.5 collective-permute-start.4
  74.3 4.5 %all-to-all-done.4 = bf16[4,128,256]{2,1,0:T(8,128)(2,1)S(1)} async-done(((bf16[4,128,256]{2,1,0:T(8,128)(2,1)}), bf16[4,128,256]{2,1,0:T(8,128)(2,1)S(1)}, u32[]{:S(2)}, u32[]{:S(2)}) %all-to-all-start.4) | async-done | bytes 262176 | tf_op jit(solution)/shard_map/all_to_all | solution.py:129
  78.8 0.2 copy.141
  79.0 0.9 copy.159
  79.9 3.4 %all-to-all-start.5 = ((bf16[4,128,256]{2,1,0:T(8,128)(2,1)}), bf16[4,128,256]{2,1,0:T(8,128)(2,1)S(1)}, u32[]{:S(2)}, u32[]{:S(2)}) async-start(bf16[4,128,256]{2,1,0:T(8,128)(2,1)} %bitcast.61), calls=%async_computation.5 | async-start | bytes 524288 | tf_op jit(solution)/shard_map/all_to_all | solution.py:132
  83.3 1.7 %collective-permute-start.6 = (bf16[128,256]{1,0:T(8,128)(2,1)S(1)}, bf16[128,256]{1,0:T(8,128)(2,1)S(1)}, u32[]{:S(2)}, u32[]{:S(2)}) collective-permute-start(bf16[128,256]{1,0:T(8,128)(2,1)S(1)} %get-tuple-element.103), channel_id=1, source_target_pairs={{0,3},{1,2},{2,1},{3,0},{4,7},{5,6},{6,5},{7,4},{8,11},{9,10},{10,... | collective-permute-start | bytes 196616 | tf_op jit(solution)/shard_map/ppermute | solution.py:21
  85.0 0.4 collective-permute-start.5
  85.4 6.7 %collective-permute-done.5 = bf16[128,256]{1,0:T(8,128)(2,1)S(1)} collective-permute-done((bf16[128,256]{1,0:T(8,128)(2,1)S(1)}, bf16[128,256]{1,0:T(8,128)(2,1)S(1)}, u32[]{:S(2)}, u32[]{:S(2)}) %collective-permute-start.5) | collective-permute-done | bytes 65568 | tf_op jit(solution)/shard_map/ppermute | solution.py:21
  92.2 0.8 copy.178
  (67 shorter events, 1.9 us)
Async XLA Ops:
  0.6 5.6 %copy-start.2 = (bf16[128,1024]{1,0:T(8,128)(2,1)S(1)}, bf16[128,1024]{1,0:T(8,128)(2,1)}, u32[]{:S(2)}) copy-start(bf16[128,1024]{1,0:T(8,128)(2,1)} %param.17) | copy-start | bytes 786436
  0.6 6.4 %copy-start.3 = (bf16[128,1024]{1,0:T(8,128)(2,1)S(1)}, bf16[128,1024]{1,0:T(8,128)(2,1)}, u32[]{:S(2)}) copy-start(bf16[128,1024]{1,0:T(8,128)(2,1)} %param.19) | copy-start | bytes 786436
  1.8 6.3 %copy-start.14 = (s32[4]{0:T(128)S(1)}, s32[4]{0:T(128)}, u32[]{:S(2)}) copy-start(s32[4]{0:T(128)} %param.21) | copy-start | bytes 52
  2.7 9.4 %all-to-all-start = ((bf16[128,4,256]{2,0,1:T(8,128)(2,1)}), bf16[128,4,256]{2,0,1:T(8,128)(2,1)S(1)}, u32[]{:S(2)}, u32[]{:S(2)}) async-start(bf16[128,4,256]{2,0,1:T(8,128)(2,1)} %copy.119), calls=%async_computation | async-start | bytes 524288 | tf_op jit(solution)/shard_map/all_to_all | solution.py:112
  6.2 18.9 %copy-start.4 = (bf16[128,1024]{1,0:T(8,128)(2,1)S(1)}, bf16[128,1024]{1,0:T(8,128)(2,1)}, u32[]{:S(2)}) copy-start(bf16[128,1024]{1,0:T(8,128)(2,1)} %param.20) | copy-start | bytes 786436
  12.1 9.4 %all-to-all-start.1 = ((bf16[128,4,256]{2,0,1:T(8,128)(2,1)}), bf16[128,4,256]{2,0,1:T(8,128)(2,1)S(1)}, u32[]{:S(2)}, u32[]{:S(2)}) async-start(bf16[128,4,256]{2,0,1:T(8,128)(2,1)} %copy.121), calls=%async_computation.1 | async-start | bytes 524288 | tf_op jit(solution)/shard_map/all_to_all | solution.py:113
  21.5 10.7 %all-to-all-start.2 = ((bf16[128,4,256]{0,2,1:T(8,128)(2,1)}), bf16[128,4,256]{0,2,1:T(8,128)(2,1)S(1)}, u32[]{:S(2)}, u32[]{:S(2)}) async-start(bf16[128,4,256]{0,2,1:T(8,128)(2,1)} %bitcast.9), calls=%async_computation.2 | async-start | bytes 524288 | tf_op jit(solution)/shard_map/all_to_all | solution.py:111
  26.4 15.3 %collective-permute-start = (bf16[64,512]{0,1:T(8,128)(2,1)S(1)}, bf16[64,512]{0,1:T(8,128)(2,1)S(1)}, u32[]{:S(2)}, u32[]{:S(2)}) collective-permute-start(bf16[64,512]{0,1:T(8,128)(2,1)S(1)} %get-tuple-element.101), channel_id=1, source_target_pairs={{0,4},{4,8},{8,12},{12,16},{16,20},{20,24},{24,28},{1,5},{5,9},{9,... | collective-permute-start | bytes 196616 | tf_op jit(solution)/shard_map/ppermute | solution.py:31
  27.7 14.0 %collective-permute-start.1 = (bf16[64,512]{0,1:T(8,128)(2,1)S(1)}, bf16[64,512]{0,1:T(8,128)(2,1)S(1)}, u32[]{:S(2)}, u32[]{:S(2)}) collective-permute-start(bf16[64,512]{0,1:T(8,128)(2,1)S(1)} %get-tuple-element.102), channel_id=1, source_target_pairs={{4,0},{8,4},{12,8},{16,12},{20,16},{24,20},{28,24},{5,1},{9,5},{13... | collective-permute-start | bytes 196616 | tf_op jit(solution)/shard_map/ppermute | solution.py:34
  32.3 9.4 %all-to-all-start.3 = ((bf16[128,4,256]{0,2,1:T(8,128)(2,1)}), bf16[128,4,256]{0,2,1:T(8,128)(2,1)S(1)}, u32[]{:S(2)}, u32[]{:S(2)}) async-start(bf16[128,4,256]{0,2,1:T(8,128)(2,1)} %bitcast.14), calls=%async_computation.3 | async-start | bytes 524288 | tf_op jit(solution)/shard_map/all_to_all | solution.py:114
  47.9 0.9 copy-start.6
  47.9 0.9 copy-start.11
  47.9 0.9 copy-start.13
  48.7 1.2 %copy-start.1 = (f32[4,128,256]{1,2,0:T(8,128)}, f32[4,128,256]{1,2,0:T(8,128)S(1)}, u32[]{:S(2)}) copy-start(f32[4,128,256]{1,2,0:T(8,128)S(1)} %fusion.127) | copy-start | bytes 1572868
  49.2 0.8 copy-start.15
  50.0 0.8 copy-start.9
  50.0 0.8 copy-start.12
  50.7 2.0 %copy-start = (f32[4,128,256]{1,2,0:T(8,128)}, f32[4,128,256]{1,2,0:T(8,128)S(1)}, u32[]{:S(2)}) copy-start(f32[4,128,256]{1,2,0:T(8,128)S(1)} %fusion.126) | copy-start | bytes 1572868
  55.1 1.5 %copy-start.7 = (bf16[256,256]{0,1:T(8,128)(2,1)S(1)}, bf16[256,256]{0,1:T(8,128)(2,1)}, u32[]{:S(2)}) copy-start(bf16[256,256]{0,1:T(8,128)(2,1)} %get-tuple-element.115) | copy-start | bytes 393220
  55.1 7.1 %collective-permute-start.2 = (f32[64,512]{1,0:T(8,128)S(1)}, f32[64,512]{1,0:T(8,128)S(1)}, u32[]{:S(2)}, u32[]{:S(2)}) collective-permute-start(f32[64,512]{1,0:T(8,128)S(1)} %slice.255), channel_id=1, source_target_pairs={{0,4},{4,8},{8,12},{12,16},{16,20},{20,24},{24,28},{1,5},{5,9},{9,... | collective-permute-start | bytes 393224 | tf_op jit(solution)/shard_map/ppermute | solution.py:42
  62.2 6.3 %copy-start.8 = (bf16[4,64,128]{2,1,0:T(8,128)(2,1)S(1)}, bf16[4,64,128]{2,1,0:T(8,128)(2,1)}, u32[]{:S(2)}) copy-start(bf16[4,64,128]{2,1,0:T(8,128)(2,1)} %convolution_convert_fusion.3) | copy-start | bytes 196612
  62.2 6.3 %copy-start.10 = (bf16[4,64,128]{2,1,0:T(8,128)(2,1)S(1)}, bf16[4,64,128]{2,1,0:T(8,128)(2,1)}, u32[]{:S(2)}) copy-start(bf16[4,64,128]{2,1,0:T(8,128)(2,1)} %convolution_convert_fusion.2) | copy-start | bytes 196612
  62.2 10.6 %collective-permute-start.3 = (f32[64,512]{1,0:T(8,128)S(1)}, f32[64,512]{1,0:T(8,128)S(1)}, u32[]{:S(2)}, u32[]{:S(2)}) collective-permute-start(f32[64,512]{1,0:T(8,128)S(1)} %get-tuple-element.91), channel_id=1, source_target_pairs={{4,0},{8,4},{12,8},{16,12},{20,16},{24,20},{28,24},{5,1},{9,5},{13... | collective-permute-start | bytes 393224 | tf_op jit(solution)/shard_map/ppermute | solution.py:42
  69.4 9.4 %all-to-all-start.4 = ((bf16[4,128,256]{2,1,0:T(8,128)(2,1)}), bf16[4,128,256]{2,1,0:T(8,128)(2,1)S(1)}, u32[]{:S(2)}, u32[]{:S(2)}) async-start(bf16[4,128,256]{2,1,0:T(8,128)(2,1)} %bitcast.42), calls=%async_computation.4 | async-start | bytes 524288 | tf_op jit(solution)/shard_map/all_to_all | solution.py:129
  73.8 11.6 %collective-permute-start.4 = (bf16[128,256]{1,0:T(8,128)(2,1)S(1)}, bf16[128,256]{1,0:T(8,128)(2,1)S(1)}, u32[]{:S(2)}, u32[]{:S(2)}) collective-permute-start(bf16[128,256]{1,0:T(8,128)(2,1)S(1)} %get-tuple-element.105), channel_id=1, source_target_pairs={{0,1},{1,0},{2,3},{3,2},{4,5},{5,4},{6,7},{7,6},{8,9},{9,8},{10,11... | collective-permute-start | bytes 196616 | tf_op jit(solution)/shard_map/ppermute | solution.py:21
  79.9 12.3 %all-to-all-start.5 = ((bf16[4,128,256]{2,1,0:T(8,128)(2,1)}), bf16[4,128,256]{2,1,0:T(8,128)(2,1)S(1)}, u32[]{:S(2)}, u32[]{:S(2)}) async-start(bf16[4,128,256]{2,1,0:T(8,128)(2,1)} %bitcast.61), calls=%async_computation.5 | async-start | bytes 524288 | tf_op jit(solution)/shard_map/all_to_all | solution.py:132
  83.3 8.8 %collective-permute-start.6 = (bf16[128,256]{1,0:T(8,128)(2,1)S(1)}, bf16[128,256]{1,0:T(8,128)(2,1)S(1)}, u32[]{:S(2)}, u32[]{:S(2)}) collective-permute-start(bf16[128,256]{1,0:T(8,128)(2,1)S(1)} %get-tuple-element.103), channel_id=1, source_target_pairs={{0,3},{1,2},{2,1},{3,0},{4,7},{5,6},{6,5},{7,4},{8,11},{9,10},{10,... | collective-permute-start | bytes 196616 | tf_op jit(solution)/shard_map/ppermute | solution.py:21
  85.0 7.1 %collective-permute-start.5 = (bf16[128,256]{1,0:T(8,128)(2,1)S(1)}, bf16[128,256]{1,0:T(8,128)(2,1)S(1)}, u32[]{:S(2)}, u32[]{:S(2)}) collective-permute-start(bf16[128,256]{1,0:T(8,128)(2,1)S(1)} %get-tuple-element.104), channel_id=1, source_target_pairs={{0,2},{1,3},{2,0},{3,1},{4,6},{5,7},{6,4},{7,5},{8,10},{9,11},{10,... | collective-permute-start | bytes 196616 | tf_op jit(solution)/shard_map/ppermute | solution.py:21
  92.1 0.8 copy-start.5
